TPU v7x, 32 devices: a whole 2x2x4 slice. The times are simulated.
32 devices in a mesh: replica: 8 (over z, core), shard: 4 (over y, x).
Axes of the slice: x: 2, y: 2, z: 4, core: 2. Of those that a mesh axis runs over, the one named last changes fastest.
Arguments:
- hidden_in: bfloat16 [4, 2048, 2048], P('shard', 'replica'), may hold values from -6 to 6
- piece_index: int32 [4, 2048], P('shard', 'replica'), may hold values from -1 to 7, as said below
- pad_flags: int32 [4, 2048], P('shard', 'replica'), may hold values from 0 to 1, as said below
- cotangent: bfloat16 [4, 2048, 2048], P('shard', 'replica'), may hold values from -6 to 6
- query_weight: bfloat16 [2048, 2048], P('shard'), may hold values from -0.125 to 0.125
- key_weight: bfloat16 [2048, 2048], P('shard'), may hold values from -0.125 to 0.125
- value_weight: bfloat16 [2048, 2048], P('shard'), may hold values from -0.125 to 0.125
- output_weight: bfloat16 [2048, 2048], P('shard'), may hold values from -0.125 to 0.125
- gate_weight: bfloat16 [2048, 8192], P('shard'), may hold values from -0.125 to 0.125
- up_weight: bfloat16 [2048, 8192], P('shard'), may hold values from -0.125 to 0.125
- down_weight: bfloat16 [8192, 2048], P('shard'), may hold values from -0.0625 to 0.0625
- query_gain: bfloat16 [2048], P('shard'), may hold values from 0.25 to 1.75
- key_gain: bfloat16 [2048], P('shard'), may hold values from 0.25 to 1.75
- attention_gain: bfloat16 [2048], P('shard'), may hold values from 0.25 to 1.75
- feed_gain: bfloat16 [2048], P('shard'), may hold values from 0.25 to 1.75
Outputs:
- result: float32 [4, 2048, 2048], P('shard', 'replica')
- grad_hidden: float32 [4, 2048, 2048], P('shard', 'replica')
- grad_query_weight: float32 [2048, 2048], P('shard')
- grad_key_weight: float32 [2048, 2048], P('shard')
- grad_value_weight: float32 [2048, 2048], P('shard')
- grad_output_weight: float32 [2048, 2048], P('shard')
- grad_gate_weight: float32 [2048, 8192], P('shard')
- grad_up_weight: float32 [2048, 8192], P('shard')
- grad_down_weight: float32 [8192, 2048], P('shard')
- grad_query_gain: float32 [2048], P('shard')
- grad_key_gain: float32 [2048], P('shard')
- grad_attention_gain: float32 [2048], P('shard')
- grad_feed_gain: float32 [2048], P('shard')
- stats: float32 [3], replicated
Inputs may be any that keep to these rules, and one draw needn't show every extreme that they name: `piece_index`: -1 marks text. A picture piece is an aligned run of 256 tokens of one sequence, all holding that run's index within the sequence; the first run of every sequence is text and the last run of every sequence is a picture piece. `pad_flags`: each sequence ends in a run of one or more padded tokens and has none elsewhere.
All inputs are finite; a program needn't handle non-finite values.
Results may differ from a plain program's by a relative error of at most 0.025.
Values may be sent and summed in bfloat16 or wider, within the bound.
No kernel may reach another device: no remote copies, remote signals or barrier semaphores. Data moves between devices by JAX's collectives and lax.ppermute only.
A program may use at most 576 MiB of HBM per device.

v0:
```python
import math
import jax
import jax.numpy as jnp
from jax import lax
from jax.sharding import PartitionSpec as P

HEADS = 16
HEAD = 128
epsilon = 1e-06
theta_base = 500000.0
masked_score = -1e30


def norm_rows(values, gain):
    scaled = values * lax.rsqrt(jnp.mean(values * values, axis=-1, keepdims=True) + epsilon)
    return scaled * gain


def angle_table(positions):
    half_head = HEAD // 2
    rates = theta_base ** (-jnp.arange(half_head).astype(jnp.float32) * (2.0 / HEAD))
    angles = positions.astype(jnp.float32)[:, None] * rates[None, :]
    return (jnp.cos(angles), jnp.sin(angles))


def rotate(values, cosine, sine):
    half_head = HEAD // 2
    first_half = values[..., :half_head]
    second_half = values[..., half_head:]
    cos_wide = cosine[:, None, :]
    sin_wide = sine[:, None, :]
    return jnp.concatenate(
        [
            first_half * cos_wide - second_half * sin_wide,
            second_half * cos_wide + first_half * sin_wide,
        ],
        axis=-1,
    )


def turn_heads(flat_rows, gain, cosine, sine):
    rows_here = flat_rows.shape[0]
    normed = norm_rows(flat_rows, gain).reshape(rows_here, HEADS, HEAD)
    return rotate(normed, cosine, sine).reshape(rows_here, HEADS * HEAD)


def contract_rows(left, right):
    return lax.dot_general(
        left, right, (((0,), (0,)), ((), ())), preferred_element_type=jnp.float32
    )


def contract_cols(left, right):
    return lax.dot_general(
        left, right, (((1,), (1,)), ((), ())), preferred_element_type=jnp.float32
    )


def block_scores(queries, keys_part, info_part, query_place, query_piece, start_key):
    rows_here = queries.shape[0]
    block_rows = keys_part.shape[0]
    scores = jnp.einsum(
        "qhd,khd->hqk",
        queries.reshape(rows_here, HEADS, HEAD),
        keys_part.reshape(block_rows, HEADS, HEAD),
        preferred_element_type=jnp.float32,
    ) * HEAD ** (-0.5)
    key_place = start_key + jnp.arange(block_rows, dtype=jnp.int32)
    key_piece = info_part.astype(jnp.float32)
    allowed = (key_place[None, :] <= query_place[:, None]) | (query_piece[:, None] >= 0.0) & (
        query_piece[:, None] == key_piece[None, :]
    )
    allowed = allowed & (key_piece[None, :] > -1.5)
    return jnp.where(allowed[None], scores, masked_score)


def per_device(
    hidden_in,
    piece_index,
    pad_flags,
    cotangent,
    query_weight,
    key_weight,
    value_weight,
    output_weight,
    gate_weight,
    up_weight,
    down_weight,
    query_gain,
    key_gain,
    attention_gain,
    feed_gain,
):
    tokens = hidden_in[0]
    rows_here = tokens.shape[0]
    width_all = tokens.shape[1]
    hidden_all = gate_weight.shape[1]
    seq_len = rows_here * lax.axis_size("replica")
    first_row = lax.axis_index("replica") * rows_here
    positions = first_row + jnp.arange(rows_here, dtype=jnp.int32)
    cosine, sine = angle_table(positions)
    score_scale = HEAD ** (-0.5)
    input_whole = ()
    feed_whole = ()
    start = jnp.int32(0)
    whole_in = input_whole
    piece_query = lax.all_gather(query_weight, "shard", axis=0, tiled=True)
    piece_key = lax.all_gather(key_weight, "shard", axis=0, tiled=True)
    piece_value = lax.all_gather(value_weight, "shard", axis=0, tiled=True)
    piece_out = lax.all_gather(output_weight, "shard", axis=0, tiled=True)
    gain_one = lax.all_gather(query_gain, "shard", axis=0, tiled=True)
    gain_two = lax.all_gather(key_gain, "shard", axis=0, tiled=True)
    gain_three = lax.all_gather(attention_gain, "shard", axis=0, tiled=True)
    gain_four = lax.all_gather(feed_gain, "shard", axis=0, tiled=True)
    columns = tokens
    sums = tuple(
        (
            jnp.dot(columns, piece, preferred_element_type=jnp.float32)
            for piece in (piece_query, piece_key, piece_value)
        )
    )
    stacked = jnp.stack([gain_one, gain_two, gain_three, gain_four])
    gain_rows = stacked
    whole_in = tuple(
        (
            lax.dynamic_update_slice_in_dim(whole, piece, start, 0)
            for whole, piece in zip(whole_in, (piece_query, piece_key, piece_value))
        )
    )
    (query_raw, key_raw, value_raw), out_whole, gain_rows, input_whole = (
        sums,
        piece_out,
        gain_rows,
        whole_in,
    )
    gains_wide = gain_rows.astype(jnp.float32)

    def turn_local(raw_rows, gain):
        return turn_heads(raw_rows, gain, cosine, sine)

    query_turned, query_pull = jax.vjp(turn_local, query_raw, gains_wide[0])
    key_turned, key_pull = jax.vjp(turn_local, key_raw, gains_wide[1])
    query_low = query_turned.astype(jnp.bfloat16)
    key_low = key_turned.astype(jnp.bfloat16)
    value_low = value_raw.astype(jnp.bfloat16)
    key_info = jnp.where(pad_flags[0] > 0, -2, piece_index[0]).astype(jnp.bfloat16)
    keys_all, values_all, info_all = (
        lax.all_gather(key_low, "replica", axis=0, tiled=True),
        lax.all_gather(value_low, "replica", axis=0, tiled=True),
        lax.all_gather(key_info, "replica", axis=0, tiled=True),
    )
    query_piece = piece_index[0].astype(jnp.float32)
    block_rows = math.gcd(seq_len, 512)
    block_count = seq_len // block_rows

    def scores_at(index):
        start_key = index * block_rows
        keys_part = lax.dynamic_slice_in_dim(keys_all, start_key, block_rows, 0)
        info_part = lax.dynamic_slice_in_dim(info_all, start_key, block_rows, 0)
        return block_scores(query_low, keys_part, info_part, positions, query_piece, start_key)

    def bound_step(index, carried):
        highest, summed = carried
        scores = scores_at(index)
        raised = jnp.maximum(highest, jnp.max(scores, axis=-1))
        summed = summed * jnp.exp(highest - raised) + jnp.sum(
            jnp.exp(scores - raised[..., None]), axis=-1
        )
        return (raised, summed)

    highest, summed = lax.fori_loop(
        0,
        block_count,
        bound_step,
        (
            jnp.full((HEADS, rows_here), masked_score, jnp.float32),
            jnp.zeros((HEADS, rows_here), jnp.float32),
        ),
    )
    log_total = highest + jnp.log(summed)

    def value_step(index, carried):
        start_key = index * block_rows
        weights_low = jnp.exp(scores_at(index) - log_total[..., None]).astype(jnp.bfloat16)
        values_part = lax.dynamic_slice_in_dim(values_all, start_key, block_rows, 0).reshape(
            block_rows, HEADS, HEAD
        )
        return carried + jnp.einsum(
            "hqk,khd->qhd", weights_low, values_part, preferred_element_type=jnp.float32
        )

    mixed = lax.fori_loop(
        0, block_count, value_step, jnp.zeros((rows_here, HEADS, HEAD), jnp.float32)
    )
    attended_low = mixed.reshape(rows_here, width_all).astype(jnp.bfloat16)
    branch_attn = jnp.dot(attended_low, out_whole, preferred_element_type=jnp.float32)
    normed_attn, attn_pull = jax.vjp(norm_rows, branch_attn, gains_wide[2])
    residual = tokens.astype(jnp.float32) + normed_attn
    residual_low = residual.astype(jnp.bfloat16)
    pieces = (
        lax.all_gather(gate_weight, "shard", axis=0, tiled=True),
        lax.all_gather(up_weight, "shard", axis=0, tiled=True),
    )
    start = jnp.int32(0)
    whole_list = feed_whole
    columns = residual_low
    sums = tuple((jnp.dot(columns, piece, preferred_element_type=jnp.float32) for piece in pieces))
    whole_list = tuple(
        (
            lax.dynamic_update_slice_in_dim(whole, piece, start, 0)
            for whole, piece in zip(whole_list, pieces)
        )
    )
    (gate_sum, up_sum), feed_whole = (sums, whole_list)

    def activate(gate_values, up_values):
        return jax.nn.silu(gate_values) * up_values

    activated, act_pull = jax.vjp(activate, gate_sum, up_sum)
    activated_low = activated.astype(jnp.bfloat16)
    piece = lax.all_gather(down_weight, "shard", axis=0, tiled=True)
    columns = activated_low
    partial_sum = jnp.dot(columns, piece, preferred_element_type=jnp.float32)
    normed_feed, feed_pull = jax.vjp(norm_rows, partial_sum, gains_wide[3])
    result = residual + normed_feed
    grad_out = cotangent[0].astype(jnp.float32)
    grad_feed, grad_feed_gain = feed_pull(grad_out)
    grad_feed_low = grad_feed.astype(jnp.bfloat16)
    grad_act = contract_cols(
        grad_feed_low, lax.all_gather(down_weight, "shard", axis=0, tiled=True)
    )
    down_share = lax.psum_scatter(
        contract_rows(activated_low, grad_feed_low).astype(jnp.bfloat16),
        "shard",
        scatter_dimension=0,
        tiled=True,
    ).astype(jnp.float32)
    grad_gate, grad_up = act_pull(grad_act)
    grad_gate_low = grad_gate.astype(jnp.bfloat16)
    grad_up_low = grad_up.astype(jnp.bfloat16)
    pieces = (
        lax.all_gather(gate_weight, "shard", axis=0, tiled=True),
        lax.all_gather(up_weight, "shard", axis=0, tiled=True),
    )
    part_sum = contract_cols(grad_gate_low, pieces[0]) + contract_cols(grad_up_low, pieces[1])
    grad_feed_in = part_sum
    grad_both = jnp.concatenate([grad_gate_low, grad_up_low], axis=1)
    feed_share = lax.psum_scatter(
        contract_rows(residual_low, grad_both).astype(jnp.bfloat16),
        "shard",
        scatter_dimension=0,
        tiled=True,
    ).astype(jnp.float32)
    grad_resid = grad_out + grad_feed_in
    grad_branch, grad_attention_gain = attn_pull(grad_resid)
    grad_branch_low = grad_branch.astype(jnp.bfloat16)
    grad_attended = contract_cols(
        grad_branch_low, lax.all_gather(output_weight, "shard", axis=0, tiled=True)
    )
    grad_mixed = grad_attended.astype(jnp.bfloat16).reshape(rows_here, HEADS, HEAD)
    delta = jnp.einsum("qhd,qhd->hq", grad_mixed.astype(jnp.float32), mixed)
    query_heads = query_low.reshape(rows_here, HEADS, HEAD)

    def back_step(index, carried):
        grad_query, grad_keys, grad_values = carried
        start_key = index * block_rows
        probs = jnp.exp(scores_at(index) - log_total[..., None])
        keys_part = lax.dynamic_slice_in_dim(keys_all, start_key, block_rows, 0).reshape(
            block_rows, HEADS, HEAD
        )
        values_part = lax.dynamic_slice_in_dim(values_all, start_key, block_rows, 0).reshape(
            block_rows, HEADS, HEAD
        )
        value_share = jnp.einsum(
            "hqk,qhd->khd",
            probs.astype(jnp.bfloat16),
            grad_mixed,
            preferred_element_type=jnp.float32,
        )
        grad_probs = jnp.einsum(
            "qhd,khd->hqk", grad_mixed, values_part, preferred_element_type=jnp.float32
        )
        grad_scores = (probs * (grad_probs - delta[..., None])).astype(jnp.bfloat16)
        grad_query = grad_query + jnp.einsum(
            "hqk,khd->qhd", grad_scores, keys_part, preferred_element_type=jnp.float32
        )
        key_share = (
            jnp.einsum("hqk,qhd->khd", grad_scores, query_heads, preferred_element_type=jnp.float32)
            * score_scale
        )
        grad_keys = lax.dynamic_update_slice_in_dim(
            grad_keys, key_share.reshape(block_rows, width_all), start_key, 0
        )
        grad_values = lax.dynamic_update_slice_in_dim(
            grad_values, value_share.reshape(block_rows, width_all), start_key, 0
        )
        return (grad_query, grad_keys, grad_values)

    zero_keys = jnp.zeros((seq_len, width_all), jnp.float32)
    grad_query, grad_keys, grad_values = lax.fori_loop(
        0,
        block_count,
        back_step,
        (jnp.zeros((rows_here, HEADS, HEAD), jnp.float32), zero_keys, zero_keys),
    )
    key_sum, value_sum = (
        lax.psum_scatter(
            grad_keys.astype(jnp.bfloat16), "replica", scatter_dimension=0, tiled=True
        ).astype(jnp.float32),
        lax.psum_scatter(
            grad_values.astype(jnp.bfloat16), "replica", scatter_dimension=0, tiled=True
        ).astype(jnp.float32),
    )
    grad_query_raw, grad_query_gain = query_pull(
        (grad_query * score_scale).reshape(rows_here, width_all)
    )
    grad_key_raw, grad_key_gain = key_pull(key_sum)
    query_back_low = grad_query_raw.astype(jnp.bfloat16)
    key_back_low = grad_key_raw.astype(jnp.bfloat16)
    value_back_low = value_sum.astype(jnp.bfloat16)
    pieces = (
        lax.all_gather(query_weight, "shard", axis=0, tiled=True),
        lax.all_gather(key_weight, "shard", axis=0, tiled=True),
        lax.all_gather(value_weight, "shard", axis=0, tiled=True),
    )
    part_sum = (
        contract_cols(query_back_low, pieces[0])
        + contract_cols(key_back_low, pieces[1])
        + contract_cols(value_back_low, pieces[2])
    )
    grad_tokens = grad_resid + part_sum
    grad_inputs = jnp.concatenate([query_back_low, key_back_low, value_back_low], axis=1)
    input_share = lax.psum_scatter(
        jnp.concatenate(
            [contract_rows(tokens, grad_inputs), contract_rows(attended_low, grad_branch_low)],
            axis=1,
        ).astype(jnp.bfloat16),
        "shard",
        scatter_dimension=0,
        tiled=True,
    ).astype(jnp.float32)
    input_share, feed_share, down_share = (
        lax.psum(input_share.astype(jnp.bfloat16), "replica").astype(jnp.float32),
        lax.psum(feed_share.astype(jnp.bfloat16), "replica").astype(jnp.float32),
        lax.psum(down_share.astype(jnp.bfloat16), "replica").astype(jnp.float32),
    )
    valid = (pad_flags[0] == 0).astype(jnp.float32)[:, None]
    stat_terms = jnp.stack(
        [
            jnp.sum(valid * result * result),
            jnp.sum(valid * branch_attn * branch_attn),
            jnp.sum(valid * partial_sum * partial_sum),
            jnp.sum(valid),
        ]
    )
    gain_terms = jnp.stack([grad_query_gain, grad_key_gain, grad_attention_gain, grad_feed_gain])
    gain_terms, stat_terms = lax.psum((gain_terms, stat_terms), ("replica", "shard"))
    gain_width = query_gain.shape[0]
    gain_mine = lax.dynamic_slice_in_dim(
        gain_terms, lax.axis_index("shard") * gain_width, gain_width, 1
    )
    stats = jnp.sqrt(stat_terms[:3] / (stat_terms[3] * width_all))
    return (
        result[None],
        grad_tokens[None],
        input_share[:, :width_all],
        input_share[:, width_all : 2 * width_all],
        input_share[:, 2 * width_all : 3 * width_all],
        input_share[:, 3 * width_all :],
        feed_share[:, :hidden_all],
        feed_share[:, hidden_all:],
        down_share,
        gain_mine[0],
        gain_mine[1],
        gain_mine[2],
        gain_mine[3],
        stats,
    )


def solution(mesh):
    placed = (
        P("shard", "replica", None),
        P("shard", "replica"),
        P("shard", "replica"),
        P("shard", "replica", None),
        P("shard", None),
        P("shard", None),
        P("shard", None),
        P("shard", None),
        P("shard", None),
        P("shard", None),
        P("shard", None),
        P("shard"),
        P("shard"),
        P("shard"),
        P("shard"),
    )
    return jax.shard_map(
        per_device,
        mesh=mesh,
        in_specs=placed,
        out_specs=(
            P("shard", "replica", None),
            P("shard", "replica", None),
            P("shard", None),
            P("shard", None),
            P("shard", None),
            P("shard", None),
            P("shard", None),
            P("shard", None),
            P("shard", None),
            P("shard"),
            P("shard"),
            P("shard"),
            P("shard"),
            P(),
        ),
        check_vma=False,
    )
```

profile of v0, /device:TPU:0, one launch (start us, length us, event | category | flops | bytes accessed | tf_op | source)
XLA Modules:
  0.0 3683.2 jit_solution(10131605898892978450)
XLA Ops:
  9.5 90.7 %all-gather.15.cloned.1.call-done = bf16[2048,2048]{1,0:T(8,128)(2,1)} async-done(((bf16[512,2048]{1,0:T(8,128)(2,1)}), bf16[2048,2048]{1,0:T(8,128)(2,1)}) %all-gather.15.cloned.1.call-update) | async-done | bytes 8388624 | tf_op jit(solution)/shard_map/all_gather | solution.py:109
  138.4 51.5 %all-gather.19.cloned.1.call-done = bf16[2048,2048]{1,0:T(8,128)(2,1)} async-done(((bf16[512,2048]{1,0:T(8,128)(2,1)}), bf16[2048,2048]{1,0:T(8,128)(2,1)}) %all-gather.19.cloned.1.call-update) | async-done | bytes 8388624 | tf_op jit(solution)/shard_map/all_gather | solution.py:108
  205.4 11.7 all-gather
  217.7 61.7 %all-gather.23.cloned.1.call-done = bf16[2048,2048]{1,0:T(8,128)(2,1)} async-done(((bf16[512,2048]{1,0:T(8,128)(2,1)}), bf16[2048,2048]{1,0:T(8,128)(2,1)}) %all-gather.23.cloned.1.call-update) | async-done | bytes 8388624 | tf_op jit(solution)/shard_map/all_gather | solution.py:107
  291.6 71.9 %all-gather.17.cloned.1.call-done = bf16[2048,2048]{1,0:T(8,128)(2,1)} async-done(((bf16[256,2048]{1,0:T(8,128)(2,1)}), bf16[2048,2048]{1,0:T(8,128)(2,1)}) %all-gather.17.cloned.1.call-update) | async-done | bytes 8388624 | tf_op jit(solution)/shard_map/all_gather | solution.py:149
  363.5 12.3 copy.126
  375.9 70.7 %all-gather.21.cloned.1.call-done = bf16[2048,2048]{0,1:T(8,128)(2,1)} async-done(((bf16[256,2048]{0,1:T(8,128)(2,1)}), bf16[2048,2048]{0,1:T(8,128)(2,1)}) %all-gather.21.cloned.1.call-update) | async-done | bytes 8388624 | tf_op jit(solution)/shard_map/all_gather | solution.py:148
  446.6 51.6 %while.48 = (s32[]{:T(128)}, f32[16,256]{1,0:T(8,128)S(1)}, f32[16,256]{1,0:T(8,128)S(1)}, f32[256]{0:T(256)S(1)}, bf16[2048]{0:T(1024)(128)(2,1)S(1)}, /*index=...) while((s32[]{:T(128)}, f32[16,256]{1,0:T(8,128)S(1)}, ...), condition=%wide.region_5.6_spmd.clone, body=%wide.region_2.5_spmd.clone.sunk | while | flops 552229376 | bytes 24739520 | solution.py:171
  498.2 42.5 %while.49 = (s32[]{:T(128)}, f32[256,16,128]{0,2,1:T(8,128)}, bf16[2048,2048]{0,1:T(8,128)(2,1)}, f32[256]{0:T(256)S(1)}, bf16[2048]{0:T(1024)(128)(2,1)S(1)}, /...) while((s32[]{:T(128)}, f32[256,16,128]{0,2,1:T(8,128)}, ...), condition=%wide.region_7.8_spmd.clone, body=%wide.region_6.7_spmd.clone.sunk | while | flops 1083836928 | bytes 18120392 | solution.py:192
  554.1 279.1 %all-gather.27.cloned.1.call-done = bf16[2048,8192]{1,0:T(8,128)(2,1)} async-done(((bf16[512,8192]{1,0:T(8,128)(2,1)}), bf16[2048,8192]{1,0:T(8,128)(2,1)}) %all-gather.27.cloned.1.call-update) | async-done | bytes 33554448 | tf_op jit(solution)/shard_map/all_gather | solution.py:201
  833.2 22.2 fusion.92
  855.5 276.8 %all-gather.29.cloned.1.call-done = bf16[2048,8192]{1,0:T(8,128)(2,1)} async-done(((bf16[512,8192]{1,0:T(8,128)(2,1)}), bf16[2048,8192]{1,0:T(8,128)(2,1)}) %all-gather.29.cloned.1.call-update) | async-done | bytes 33554448 | tf_op jit(solution)/shard_map/all_gather | solution.py:202
  1132.3 26.9 multiply_convert_fusion.1
  1159.2 272.2 %all-gather.31.cloned.1.call-done = bf16[8192,2048]{1,0:T(8,128)(2,1)} async-done(((bf16[2048,2048]{1,0:T(8,128)(2,1)}), bf16[8192,2048]{1,0:T(8,128)(2,1)}) %all-gather.31.cloned.1.call-update) | async-done | bytes 33554448 | tf_op jit(solution)/shard_map/all_gather | solution.py:221
  1431.4 16.6 multiply_reduce_fusion.7
  1450.1 22.0 multiply_convert_fusion
  1472.1 17.1 fusion.93
  1489.2 20.5 multiply_reduce_fusion.1
  1531.4 106.4 %while.50 = (s32[]{:T(128)}, f32[256,16,128]{0,2,1:T(8,128)}, bf16[2048,2048]{0,1:T(8,128)(2,1)}, bf16[2048,2048]{1,0:T(8,128)(2,1)}, bf16[2048,2048]{0,1:T(8,12...) while((s32[]{:T(128)}, f32[256,16,128]{0,2,1:T(8,128)}, ...), condition=%wide.region_13.14_spmd.clone, body=%wide.region_12.13_spmd.clone.sunk | while | flops 2709129728 | bytes 103219016 | solution.py:300
  1639.7 16.4 convolution_convert_fusion.1
  1665.9 61.8 %reduce-scatter.10.cloned.1.call-done = bf16[256,2048]{0,1:T(8,128)(2,1)} async-done(((bf16[2048,2048]{0,1:T(8,128)(2,1)}), bf16[256,2048]{0,1:T(8,128)(2,1)}) %reduce-scatter.10.cloned.1.call-update) | async-done | bytes 1048592 | tf_op jit(solution)/shard_map/reduce_scatter | solution.py:307
  1741.6 76.9 %reduce-scatter.12.cloned.1.call-done = bf16[256,2048]{1,0:T(8,128)(2,1)} async-done(((bf16[2048,2048]{1,0:T(8,128)(2,1)}), bf16[256,2048]{1,0:T(8,128)(2,1)}) %reduce-scatter.12.cloned.1.call-update) | async-done | bytes 1048592 | tf_op jit(solution)/shard_map/reduce_scatter | solution.py:310
  1818.5 13.4 convert_bitcast_fusion
  1831.8 24.4 pad_maximum_fusion
  1857.4 29.1 convolution_convert_fusion
  1886.8 221.6 %reduce-scatter.18.cloned.1.call-done = bf16[2048,2048]{1,0:T(8,128)(2,1)} async-done(((bf16[8192,2048]{1,0:T(8,128)(2,1)}), bf16[2048,2048]{1,0:T(8,128)(2,1)}) %reduce-scatter.18.cloned.1.call-update) | async-done | bytes 8388624
  2108.4 292.0 %reduce-scatter.14.cloned.1.call-done = bf16[512,8192]{0,1:T(8,128)(2,1)} async-done(((bf16[2048,8192]{0,1:T(8,128)(2,1)}), bf16[512,8192]{0,1:T(8,128)(2,1)}) %reduce-scatter.14.cloned.1.call-update) | async-done | bytes 8388624 | tf_op jit(solution)/shard_map/reduce_scatter | solution.py:333
  2400.5 561.2 %reduce-scatter.16.cloned.1.call-done = bf16[512,16384]{1,0:T(8,128)(2,1)} async-done(((bf16[2048,16384]{1,0:T(8,128)(2,1)}), bf16[512,16384]{1,0:T(8,128)(2,1)}) %reduce-scatter.16.cloned.1.call-update) | async-done | bytes 16777232
  2965.6 41.1 %all-reduce.6 = (f32[4,2048]{1,0:T(4,128)S(1)}, f32[4]{0:T(128)S(1)}) all-reduce(f32[4,2048]{1,0:T(4,128)S(1)} %pad_maximum_fusion.2, f32[4]{0:T(128)S(1)} %pad_maximum_fusion.3), channel_id=1, replica_groups=mesh['replica'=8,'shard'=4] {'replica','shard'}, use_global_device_ids=true, to_apply=%region_28.29 | all-reduce | flops 8196 | bytes 65568 | tf_op jit(solution)/shard_map/psum | solution.py:357
  3025.0 591.2 %all-reduce.10.cloned.1.call-done = (bf16[512,8192]{0,1:T(8,128)(2,1)}, bf16[512,16384]{1,0:T(8,128)(2,1)}, bf16[2048,2048]{1,0:T(8,128)(2,1)}) async-done(((bf16[512,8192]{0,1:T(8,128)(2,1)}, bf16[512,16384]{1,0:T(8,128)(2,1)}, bf16[2048,2048]{1,0:T(8,128)(2,1)}), (bf16[512,8192]{0,1:T(8,128)(2,1)}, bf16[512,16384]{1,0:T(8,128)(2,1)}, bf16[2048,2048]{1,0:T(8,128)(2,1)})) %all-reduce.10.cloned.1.call-update) | async-done | bytes 33554448 | tf_op jit(solution)/shard_map/psum | solution.py:343
  3616.1 16.9 fusion.86
  3664.8 11.7 convert_element_type.207
  (412 shorter events, 384.8 us)
Async XLA Ops:
  7.2 93.0 %all-gather.15.cloned.1.call-start = ((), (), s32[]{:S(2)}) async-start(), calls=%async_computation.5 | async-start | bytes 10485760 | tf_op jit(solution)/shard_map/all_gather | solution.py:109
  7.9 92.3 %copy-start.22 = (bf16[1,256,2048]{2,1,0:T(8,128)(2,1)S(1)}, bf16[1,256,2048]{2,1,0:T(8,128)(2,1)}, u32[]{:S(2)}) copy-start(bf16[1,256,2048]{2,1,0:T(8,128)(2,1)} %param.21) | copy-start | bytes 3145732
  7.9 181.9 %all-gather.19.cloned.1.call-start = ((), (), s32[]{:S(2)}) async-start(), calls=%async_computation.7 | async-start | bytes 10485760 | tf_op jit(solution)/shard_map/all_gather | solution.py:108
  8.7 270.7 %all-gather.23.cloned.1.call-start = ((), (), s32[]{:S(2)}) async-start(), calls=%async_computation.9 | async-start | bytes 10485760 | tf_op jit(solution)/shard_map/all_gather | solution.py:107
  9.4 97.6 %copy-start.62 = (bf16[512]{0:T(512)(128)(2,1)S(1)}, bf16[512]{0:T(512)(128)(2,1)}, u32[]{:S(2)}) copy-start(bf16[512]{0:T(512)(128)(2,1)} %param.32) | copy-start | bytes 3076
  9.4 97.6 %copy-start.63 = (bf16[512]{0:T(512)(128)(2,1)S(1)}, bf16[512]{0:T(512)(128)(2,1)}, u32[]{:S(2)}) copy-start(bf16[512]{0:T(512)(128)(2,1)} %param.33) | copy-start | bytes 3076
  9.4 97.6 %copy-start.64 = (bf16[512]{0:T(512)(128)(2,1)S(1)}, bf16[512]{0:T(512)(128)(2,1)}, u32[]{:S(2)}) copy-start(bf16[512]{0:T(512)(128)(2,1)} %param.34) | copy-start | bytes 3076
  9.4 97.6 %copy-start.65 = (bf16[512]{0:T(512)(128)(2,1)S(1)}, bf16[512]{0:T(512)(128)(2,1)}, u32[]{:S(2)}) copy-start(bf16[512]{0:T(512)(128)(2,1)} %param.35) | copy-start | bytes 3076
  9.4 354.1 %all-gather.17.cloned.1.call-start = ((), (), s32[]{:S(2)}) async-start(), calls=%async_computation.6 | async-start | bytes 9437184 | tf_op jit(solution)/shard_map/all_gather | solution.py:149
  106.9 339.7 %all-gather.21.cloned.1.call-start = ((), (), s32[]{:S(2)}) async-start(), calls=%async_computation.8 | async-start | bytes 9437184 | tf_op jit(solution)/shard_map/all_gather | solution.py:148
  137.7 151.1 %copy-start.30 = (f32[256,64]{0,1:T(8,128)}, f32[256,64]{0,1:T(8,128)S(1)}, u32[]{:S(2)}) copy-start(f32[256,64]{0,1:T(8,128)S(1)} %get-tuple-element.949) | copy-start | bytes 196612
  137.7 151.1 %copy-start.32 = (f32[256,64]{0,1:T(8,128)}, f32[256,64]{0,1:T(8,128)S(1)}, u32[]{:S(2)}) copy-start(f32[256,64]{0,1:T(8,128)S(1)} %get-tuple-element.950) | copy-start | bytes 196612
  138.4 57.3 %copy-start.42 = (f32[1,2048]{1,0:T(1,128)}, f32[1,2048]{1,0:T(1,128)S(1)}, u32[]{:S(2)}) copy-start(f32[1,2048]{1,0:T(1,128)S(1)} %get-tuple-element.948) | copy-start | bytes 24580
  138.4 147.4 %copy-start.40 = (f32[1,2048]{1,0:T(1,128)}, f32[1,2048]{1,0:T(1,128)S(1)}, u32[]{:S(2)}) copy-start(f32[1,2048]{1,0:T(1,128)S(1)} %get-tuple-element.947) | copy-start | bytes 24580
  202.4 340.7 %all-gather.25.cloned.1.call-start = ((), (), s32[]{:S(2)}) async-start(), calls=%async_computation.10 | async-start | bytes 10485760 | tf_op jit(solution)/shard_map/all_gather | solution.py:110
  203.0 630.2 %all-gather.27.cloned.1.call-start = ((), (), s32[]{:S(2)}) async-start(), calls=%async_computation.11 | async-start | bytes 41943040 | tf_op jit(solution)/shard_map/all_gather | solution.py:201
  203.8 928.5 %all-gather.29.cloned.1.call-start = ((), (), s32[]{:S(2)}) async-start(), calls=%async_computation.12 | async-start | bytes 41943040 | tf_op jit(solution)/shard_map/all_gather | solution.py:202
  204.5 1226.8 %all-gather.31.cloned.1.call-start = ((), (), s32[]{:S(2)}) async-start(), calls=%async_computation.13 | async-start | bytes 41943040 | tf_op jit(solution)/shard_map/all_gather | solution.py:221
  205.3 1522.3 %reduce-scatter.10.cloned.1.call-start = ((), (), s32[]{:S(2)}) async-start(), calls=%async_computation.14 | async-start | bytes 9437184 | tf_op jit(solution)/shard_map/reduce_scatter | solution.py:307
  291.0 84.9 %copy-start.4 = (bf16[256,16,128]{0,2,1:T(8,128)(2,1)}, bf16[256,16,128]{0,2,1:T(8,128)(2,1)S(1)}, u32[]{:S(2)}) copy-start(bf16[256,16,128]{0,2,1:T(8,128)(2,1)S(1)} %maximum_convert_fusion) | copy-start | bytes 3145732
  554.1 578.2 %copy-start.20 = (bf16[256,2048]{1,0:T(8,128)(2,1)}, bf16[256,2048]{1,0:T(8,128)(2,1)S(1)}, u32[]{:S(2)}) copy-start(bf16[256,2048]{1,0:T(8,128)(2,1)S(1)} %fusion.71) | copy-start | bytes 3145732
  1448.0 24.1 copy-start.16
  1472.1 39.6 %slice-start = ((s8[8388608]{0:T(1024)(128)(4,1)}), s8[4194304]{0:T(1024)(128)(4,1)S(1)}, s32[]{:S(2)}) async-start(s8[8388608]{0:T(1024)(128)(4,1)} %bitcast.255), calls=%async_computation.20 | async-start | bytes 8388608
  1637.8 180.7 %reduce-scatter.12.cloned.1.call-start = ((), (), s32[]{:S(2)}) async-start(), calls=%async_computation.15 | async-start | bytes 9437184 | tf_op jit(solution)/shard_map/reduce_scatter | solution.py:310
  1638.6 469.9 %reduce-scatter.18.cloned.1.call-start = ((), (), s32[]{:S(2)}) async-start(), calls=%async_computation.18 | async-start | bytes 41943040
  1656.2 744.3 %reduce-scatter.14.cloned.1.call-start = ((), (), s32[]{:S(2)}) async-start(), calls=%async_computation.16 | async-start | bytes 41943040 | tf_op jit(solution)/shard_map/reduce_scatter | solution.py:333
  1665.8 63.2 %copy-start.19 = (f32[256,16,128]{0,2,1:T(8,128)S(1)}, f32[256,16,128]{0,2,1:T(8,128)}, u32[]{:S(2)}) copy-start(f32[256,16,128]{0,2,1:T(8,128)} %broadcast_multiply_fusion) | copy-start | bytes 6291460
  1665.8 63.2 %copy-start.31 = (f32[256,64]{0,1:T(8,128)S(1)}, f32[256,64]{0,1:T(8,128)}, u32[]{:S(2)}) copy-start(f32[256,64]{0,1:T(8,128)} %copy-done.30) | copy-start | bytes 196612
  1665.8 63.2 %copy-start.33 = (f32[256,64]{0,1:T(8,128)S(1)}, f32[256,64]{0,1:T(8,128)}, u32[]{:S(2)}) copy-start(f32[256,64]{0,1:T(8,128)} %copy-done.32) | copy-start | bytes 196612
  1741.1 77.4 %copy-start.24 = (bf16[1,256,2048]{2,1,0:T(8,128)(2,1)S(1)}, bf16[1,256,2048]{2,1,0:T(8,128)(2,1)}, u32[]{:S(2)}) copy-start(bf16[1,256,2048]{2,1,0:T(8,128)(2,1)} %param.21) | copy-start | bytes 3145732
  1856.3 1105.4 %reduce-scatter.16.cloned.1.call-start = ((), (), s32[]{:S(2)}) async-start(), calls=%async_computation.17 | async-start | bytes 83886080
  1886.5 1729.6 %all-reduce.10.cloned.1.call-start = ((), (), s32[]{:S(2)}) async-start(), calls=%async_computation.19 | async-start | bytes 67108864 | tf_op jit(solution)/shard_map/psum | solution.py:343
  (63 other events, 316.3 us)
Sparse Core Ops, SparseCore 0:
  9.9 90.2 all-gather.14
  102.0 87.7 all-gather.18
  191.7 87.6 all-gather.22
  281.4 82.0 all-gather.16
  365.5 81.0 all-gather.20
  448.3 85.7 all-gather.24
  536.0 297.2 all-gather.26
  835.1 297.2 all-gather.28
  1134.1 297.2 all-gather.30
  1638.0 89.6 reduce-scatter.9
  1730.5 87.9 reduce-scatter.11
  1821.4 286.9 reduce-scatter.17
  2111.8 288.6 reduce-scatter.13
  2403.4 558.2 reduce-scatter.15
  2964.4 651.7 all-reduce.9
where the time goes:
time: 3690 us; the launch traced here: 3680 us
  waiting for transfers between devices  2980 us (81%)
  matrix products  339 us (9%)
  local copies, waits for them, and re-layouts  166 us (4%)
  other arithmetic  92.9 us (3%)
  blocking collectives  83.1 us (2%)
    unnamed x17, waiting for transfers between devices  788 us
    psum x1, waiting for transfers between devices, per_device(): lax.psum(input_share.astype(jnp.bfloat16), 'replica').astype(jnp.float32)  591 us
    reduce_scatter x1, waiting for transfers between devices, per_device(): lax.psum_scatter(jnp.concatenate([contract_rows(tokens, grad_inputs), con...  292 us
    all_gather x1, waiting for transfers between devices, per_device(): lax.all_gather(gate_weight, 'shard', axis=0, tiled=True)  279 us
    all_gather x1, waiting for transfers between devices, per_device(): lax.all_gather(up_weight, 'shard', axis=0, tiled=True)  277 us
    all_gather x1, waiting for transfers between devices, per_device(): piece = lax.all_gather(down_weight, 'shard', axis=0, tiled=True)  272 us
    all_gather x1, waiting for transfers between devices, per_device(): piece_value = lax.all_gather(value_weight, 'shard', axis=0, tiled=True)  90.7 us
    dot_general x7, matrix products, contract_cols(): lax.dot_general(left, right, (((1,), (1,)), ((), ())), preferred_element_...  77.7 us
  transfers between devices with their start and end apart: 15, of which 14 were waited for; matrix products, arithmetic and copies ran while one was open for 9% of the time, Pallas kernels for 0%

commit v1 on v0

--- a/solution.py
+++ b/solution.py
@@ -9,6 +9,18 @@
 epsilon = 1e-06
 theta_base = 500000.0
 masked_score = -1e30
+
+
+def gather_by_bits(shard, axis, dim):
+    ways, here, step = (lax.axis_size(axis), lax.axis_index(axis), shard.shape[dim])
+    line, have = (shard, 1)
+    while have < ways:
+        line = jnp.concatenate(
+            [line, lax.ppermute(line, axis, [(d, (d - have) % ways) for d in range(ways)])],
+            axis=dim,
+        )
+        have = 2 * have
+    return jnp.roll(line, here * step, axis=dim)
 
 
 def norm_rows(values, gain):
@@ -218,7 +230,7 @@
 
     activated, act_pull = jax.vjp(activate, gate_sum, up_sum)
     activated_low = activated.astype(jnp.bfloat16)
-    piece = lax.all_gather(down_weight, "shard", axis=0, tiled=True)
+    piece = gather_by_bits(down_weight, "shard", 0)
     columns = activated_low
     partial_sum = jnp.dot(columns, piece, preferred_element_type=jnp.float32)
     normed_feed, feed_pull = jax.vjp(norm_rows, partial_sum, gains_wide[3])

time: 3690 us -> 4010 us (1.087)
  waiting for transfers between devices: 2980 us -> 3220 us
  local copies, waits for them, and re-layouts: 166 us -> 232 us
    ppermute x0 -> x2, waiting for transfers between devices: none -> 621 us  [gather_by_bits(): lax.ppermute(line, axis, [(d, (d - have) % ways) for d in range(ways)])]
    all_gather x1, waiting for transfers between devices: 279 us -> 72.4 us  [per_device(): lax.all_gather(gate_weight, 'shard', axis=0, tiled=True)]
    all_gather x1, waiting for transfers between devices: 71.9 us -> 0.01 us  [per_device(): lax.all_gather(value_low, 'replica', axis=0, tiled=True)]
    all_gather x1, waiting for transfers between devices: 70.7 us -> 0.01 us  [per_device(): lax.all_gather(key_low, 'replica', axis=0, tiled=True)]
    unnamed x149 -> x156, local copies, waits for them, and re-layouts: 49.9 us -> 94 us
  transfers between devices with their start and end apart: 15 -> 17, of which waited for: 14 -> 14; matrix products, arithmetic and copies ran while one was open for 9% -> 10% of each run, Pallas kernels for 0% -> 0%
where the time goes in v1:
time: 4010 us; the launch traced here: 4000 us
  waiting for transfers between devices  3220 us (80%)
  matrix products  337 us (8%)
  local copies, waits for them, and re-layouts  232 us (6%)
  other arithmetic  108 us (3%)
  blocking collectives  83.1 us (2%)
    unnamed x17, waiting for transfers between devices  787 us
    ppermute x2, waiting for transfers between devices, gather_by_bits(): lax.ppermute(line, axis, [(d, (d - have) % ways) for d in range(ways)])  621 us
    psum x1, waiting for transfers between devices, per_device(): lax.psum(input_share.astype(jnp.bfloat16), 'replica').astype(jnp.float32)  591 us
    reduce_scatter x1, waiting for transfers between devices, per_device(): lax.psum_scatter(jnp.concatenate([contract_rows(tokens, grad_inputs), con...  292 us
    all_gather x1, waiting for transfers between devices, per_device(): lax.all_gather(up_weight, 'shard', axis=0, tiled=True)  278 us
    all_gather x1, waiting for transfers between devices, per_device(): lax.all_gather(down_weight, 'shard', axis=0, tiled=True)  251 us
    unnamed x156, local copies, waits for them, and re-layouts  94 us
    all_gather x1, waiting for transfers between devices, per_device(): piece_value = lax.all_gather(value_weight, 'shard', axis=0, tiled=True)  90.7 us
  transfers between devices with their start and end apart: 17, of which 14 were waited for; matrix products, arithmetic and copies ran while one was open for 10% of the time, Pallas kernels for 0%

profile of v1, /device:TPU:0, one launch (start us, length us, event | category | flops | bytes accessed | tf_op | source)
XLA Modules:
  0.0 4001.9 jit_solution(4910728943096451063)
XLA Ops:
  9.5 90.7 %all-gather.15.cloned.1.call-done = bf16[2048,2048]{1,0:T(8,128)(2,1)} async-done(((bf16[512,2048]{1,0:T(8,128)(2,1)}), bf16[2048,2048]{1,0:T(8,128)(2,1)}) %all-gather.15.cloned.1.call-update) | async-done | bytes 8388624 | tf_op jit(solution)/shard_map/all_gather | solution.py:121
  138.4 51.5 %all-gather.19.cloned.1.call-done = bf16[2048,2048]{1,0:T(8,128)(2,1)} async-done(((bf16[512,2048]{1,0:T(8,128)(2,1)}), bf16[2048,2048]{1,0:T(8,128)(2,1)}) %all-gather.19.cloned.1.call-update) | async-done | bytes 8388624 | tf_op jit(solution)/shard_map/all_gather | solution.py:120
  206.0 199.7 %collective-permute-done = bf16[2048,2048]{1,0:T(8,128)(2,1)S(1)} collective-permute-done((bf16[2048,2048]{1,0:T(8,128)(2,1)}, bf16[2048,2048]{1,0:T(8,128)(2,1)S(1)}, u32[]{:S(2)}, u32[]{:S(2)}) %collective-permute-start) | collective-permute-done | bytes 8388640 | tf_op jit(solution)/shard_map/ppermute | solution.py:19
  448.5 48.9 %all-gather.23.cloned.1.call-done = bf16[2048,2048]{1,0:T(8,128)(2,1)} async-done(((bf16[512,2048]{1,0:T(8,128)(2,1)}), bf16[2048,2048]{1,0:T(8,128)(2,1)}) %all-gather.23.cloned.1.call-update) | async-done | bytes 8388624 | tf_op jit(solution)/shard_map/all_gather | solution.py:119
  509.6 421.0 %collective-permute-done.1 = bf16[4096,2048]{1,0:T(8,128)(2,1)} collective-permute-done((bf16[4096,2048]{1,0:T(8,128)(2,1)}, bf16[4096,2048]{1,0:T(8,128)(2,1)}, u32[]{:S(2)}, u32[]{:S(2)}) %collective-permute-start.1) | collective-permute-done | bytes 16777248 | tf_op jit(solution)/shard_map/ppermute | solution.py:19
  930.6 14.1 constant_dynamic-update-slice_fusion.5
  961.4 14.1 constant_dynamic-update-slice_fusion.2
  975.5 12.5 copy.126
  988.0 50.4 %while.48 = (s32[]{:T(128)}, f32[16,256]{1,0:T(8,128)S(1)}, f32[16,256]{1,0:T(8,128)S(1)}, f32[256]{0:T(256)S(1)}, bf16[2048]{0:T(1024)(128)(2,1)S(1)}, /*index=...) while((s32[]{:T(128)}, f32[16,256]{1,0:T(8,128)S(1)}, ...), condition=%wide.region_5.6_spmd.clone, body=%wide.region_2.5_spmd.clone.sunk | while | flops 552229376 | bytes 24739520 | solution.py:183
  1038.5 42.7 %while.49 = (s32[]{:T(128)}, f32[256,16,128]{0,2,1:T(8,128)}, bf16[2048,2048]{0,1:T(8,128)(2,1)}, f32[256]{0:T(256)S(1)}, bf16[2048]{0:T(1024)(128)(2,1)S(1)}, /...) while((s32[]{:T(128)}, f32[256,16,128]{0,2,1:T(8,128)}, ...), condition=%wide.region_7.8_spmd.clone, body=%wide.region_6.7_spmd.clone.sunk | while | flops 1083836928 | bytes 18120392 | solution.py:204
  1091.0 72.4 %all-gather.27.cloned.1.call-done = bf16[2048,8192]{1,0:T(8,128)(2,1)} async-done(((bf16[512,8192]{1,0:T(8,128)(2,1)}), bf16[2048,8192]{1,0:T(8,128)(2,1)}) %all-gather.27.cloned.1.call-update) | async-done | bytes 33554448 | tf_op jit(solution)/shard_map/all_gather | solution.py:213
  1163.4 21.2 fusion.95
  1184.6 277.9 %all-gather.29.cloned.1.call-done = bf16[2048,8192]{1,0:T(8,128)(2,1)} async-done(((bf16[512,8192]{1,0:T(8,128)(2,1)}), bf16[2048,8192]{1,0:T(8,128)(2,1)}) %all-gather.29.cloned.1.call-update) | async-done | bytes 33554448 | tf_op jit(solution)/shard_map/all_gather | solution.py:214
  1462.5 26.9 multiply_convert_fusion.1
  1489.4 17.7 multiply_reduce_fusion.7
  1510.5 251.0 %all-gather.31.cloned.1.call-done = bf16[8192,2048]{1,0:T(8,128)(2,1)} async-done(((bf16[2048,2048]{1,0:T(8,128)(2,1)}), bf16[8192,2048]{1,0:T(8,128)(2,1)}) %all-gather.31.cloned.1.call-update) | async-done | bytes 33554448 | tf_op jit(solution)/shard_map/all_gather | solution.py:242
  1761.6 23.3 multiply_convert_fusion
  1784.9 16.9 fusion.96
  1801.8 20.8 multiply_reduce_fusion.1
  1844.2 112.3 %while.50 = (s32[]{:T(128)}, f32[256,16,128]{0,2,1:T(8,128)}, bf16[2048,2048]{0,1:T(8,128)(2,1)}, bf16[2048,2048]{1,0:T(8,128)(2,1)}, bf16[2048,2048]{0,1:T(8,12...) while((s32[]{:T(128)}, f32[256,16,128]{0,2,1:T(8,128)}, ...), condition=%wide.region_13.14_spmd.clone, body=%wide.region_12.13_spmd.clone.sunk | while | flops 2709129728 | bytes 103219016 | solution.py:312
  1958.4 16.3 convolution_convert_fusion.1
  1983.7 62.6 %reduce-scatter.10.cloned.1.call-done = bf16[256,2048]{0,1:T(8,128)(2,1)} async-done(((bf16[2048,2048]{0,1:T(8,128)(2,1)}), bf16[256,2048]{0,1:T(8,128)(2,1)}) %reduce-scatter.10.cloned.1.call-update) | async-done | bytes 1048592 | tf_op jit(solution)/shard_map/reduce_scatter | solution.py:319
  2062.2 75.0 %reduce-scatter.12.cloned.1.call-done = bf16[256,2048]{1,0:T(8,128)(2,1)} async-done(((bf16[2048,2048]{1,0:T(8,128)(2,1)}), bf16[256,2048]{1,0:T(8,128)(2,1)}) %reduce-scatter.12.cloned.1.call-update) | async-done | bytes 1048592 | tf_op jit(solution)/shard_map/reduce_scatter | solution.py:322
  2137.2 13.3 convert_bitcast_fusion
  2150.5 25.1 pad_maximum_fusion
  2176.9 29.0 convolution_convert_fusion
  2206.2 221.0 %reduce-scatter.18.cloned.1.call-done = bf16[2048,2048]{1,0:T(8,128)(2,1)} async-done(((bf16[8192,2048]{1,0:T(8,128)(2,1)}), bf16[2048,2048]{1,0:T(8,128)(2,1)}) %reduce-scatter.18.cloned.1.call-update) | async-done | bytes 8388624
  2427.1 292.0 %reduce-scatter.14.cloned.1.call-done = bf16[512,8192]{0,1:T(8,128)(2,1)} async-done(((bf16[2048,8192]{0,1:T(8,128)(2,1)}), bf16[512,8192]{0,1:T(8,128)(2,1)}) %reduce-scatter.14.cloned.1.call-update) | async-done | bytes 8388624 | tf_op jit(solution)/shard_map/reduce_scatter | solution.py:345
  2719.1 561.2 %reduce-scatter.16.cloned.1.call-done = bf16[512,16384]{1,0:T(8,128)(2,1)} async-done(((bf16[2048,16384]{1,0:T(8,128)(2,1)}), bf16[512,16384]{1,0:T(8,128)(2,1)}) %reduce-scatter.16.cloned.1.call-update) | async-done | bytes 16777232
  3284.3 41.1 %all-reduce.6 = (f32[4,2048]{1,0:T(4,128)S(1)}, f32[4]{0:T(128)S(1)}) all-reduce(f32[4,2048]{1,0:T(4,128)S(1)} %pad_maximum_fusion.3, f32[4]{0:T(128)S(1)} %pad_maximum_fusion.4), channel_id=1, replica_groups=mesh['replica'=8,'shard'=4] {'replica','shard'}, use_global_device_ids=true, to_apply=%region_28.29 | all-reduce | flops 8196 | bytes 65568 | tf_op jit(solution)/shard_map/psum | solution.py:369
  3343.7 591.2 %all-reduce.10.cloned.1.call-done = (bf16[512,8192]{0,1:T(8,128)(2,1)}, bf16[512,16384]{1,0:T(8,128)(2,1)}, bf16[2048,2048]{1,0:T(8,128)(2,1)}) async-done(((bf16[512,8192]{0,1:T(8,128)(2,1)}, bf16[512,16384]{1,0:T(8,128)(2,1)}, bf16[2048,2048]{1,0:T(8,128)(2,1)}), (bf16[512,8192]{0,1:T(8,128)(2,1)}, bf16[512,16384]{1,0:T(8,128)(2,1)}, bf16[2048,2048]{1,0:T(8,128)(2,1)})) %all-reduce.10.cloned.1.call-update) | async-done | bytes 33554448 | tf_op jit(solution)/shard_map/psum | solution.py:355
  3934.8 16.9 fusion.89
  (425 shorter events, 459.7 us)
Async XLA Ops:
  7.2 93.0 %copy-start.19 = (bf16[1,256,2048]{2,1,0:T(8,128)(2,1)S(1)}, bf16[1,256,2048]{2,1,0:T(8,128)(2,1)}, u32[]{:S(2)}) copy-start(bf16[1,256,2048]{2,1,0:T(8,128)(2,1)} %param.21) | copy-start | bytes 3145732
  7.2 93.0 %all-gather.15.cloned.1.call-start = ((), (), s32[]{:S(2)}) async-start(), calls=%async_computation.5 | async-start | bytes 10485760 | tf_op jit(solution)/shard_map/all_gather | solution.py:121
  7.9 182.0 %all-gather.19.cloned.1.call-start = ((), (), s32[]{:S(2)}) async-start(), calls=%async_computation.7 | async-start | bytes 10485760 | tf_op jit(solution)/shard_map/all_gather | solution.py:120
  8.7 488.7 %all-gather.23.cloned.1.call-start = ((), (), s32[]{:S(2)}) async-start(), calls=%async_computation.9 | async-start | bytes 10485760 | tf_op jit(solution)/shard_map/all_gather | solution.py:119
  9.4 97.6 %copy-start.63 = (bf16[512]{0:T(512)(128)(2,1)S(1)}, bf16[512]{0:T(512)(128)(2,1)}, u32[]{:S(2)}) copy-start(bf16[512]{0:T(512)(128)(2,1)} %param.32) | copy-start | bytes 3076
  9.4 97.6 %copy-start.64 = (bf16[512]{0:T(512)(128)(2,1)S(1)}, bf16[512]{0:T(512)(128)(2,1)}, u32[]{:S(2)}) copy-start(bf16[512]{0:T(512)(128)(2,1)} %param.33) | copy-start | bytes 3076
  9.4 97.6 %copy-start.65 = (bf16[512]{0:T(512)(128)(2,1)S(1)}, bf16[512]{0:T(512)(128)(2,1)}, u32[]{:S(2)}) copy-start(bf16[512]{0:T(512)(128)(2,1)} %param.34) | copy-start | bytes 3076
  9.4 97.6 %copy-start.66 = (bf16[512]{0:T(512)(128)(2,1)S(1)}, bf16[512]{0:T(512)(128)(2,1)}, u32[]{:S(2)}) copy-start(bf16[512]{0:T(512)(128)(2,1)} %param.35) | copy-start | bytes 3076
  9.4 966.0 %all-gather.17.cloned.1.call-start = ((), (), s32[]{:S(2)}) async-start(), calls=%async_computation.6 | async-start | bytes 9437184 | tf_op jit(solution)/shard_map/all_gather | solution.py:161
  106.9 881.1 %all-gather.21.cloned.1.call-start = ((), (), s32[]{:S(2)}) async-start(), calls=%async_computation.8 | async-start | bytes 9437184 | tf_op jit(solution)/shard_map/all_gather | solution.py:160
  137.7 369.0 %copy-start.30 = (f32[256,64]{0,1:T(8,128)}, f32[256,64]{0,1:T(8,128)S(1)}, u32[]{:S(2)}) copy-start(f32[256,64]{0,1:T(8,128)S(1)} %get-tuple-element.949) | copy-start | bytes 196612
  137.7 369.0 %copy-start.32 = (f32[256,64]{0,1:T(8,128)}, f32[256,64]{0,1:T(8,128)S(1)}, u32[]{:S(2)}) copy-start(f32[256,64]{0,1:T(8,128)S(1)} %get-tuple-element.950) | copy-start | bytes 196612
  138.4 365.4 %copy-start.40 = (f32[1,2048]{1,0:T(1,128)}, f32[1,2048]{1,0:T(1,128)S(1)}, u32[]{:S(2)}) copy-start(f32[1,2048]{1,0:T(1,128)S(1)} %get-tuple-element.947) | copy-start | bytes 24580
  202.4 881.8 %all-gather.25.cloned.1.call-start = ((), (), s32[]{:S(2)}) async-start(), calls=%async_computation.10 | async-start | bytes 10485760 | tf_op jit(solution)/shard_map/all_gather | solution.py:122
  203.0 960.4 %all-gather.27.cloned.1.call-start = ((), (), s32[]{:S(2)}) async-start(), calls=%async_computation.11 | async-start | bytes 41943040 | tf_op jit(solution)/shard_map/all_gather | solution.py:213
  203.8 1258.7 %all-gather.29.cloned.1.call-start = ((), (), s32[]{:S(2)}) async-start(), calls=%async_computation.12 | async-start | bytes 41943040 | tf_op jit(solution)/shard_map/all_gather | solution.py:214
  204.5 1557.0 %all-gather.31.cloned.1.call-start = ((), (), s32[]{:S(2)}) async-start(), calls=%async_computation.13 | async-start | bytes 41943040 | tf_op jit(solution)/shard_map/all_gather | solution.py:242
  204.6 201.2 %collective-permute-start = (bf16[2048,2048]{1,0:T(8,128)(2,1)}, bf16[2048,2048]{1,0:T(8,128)(2,1)S(1)}, u32[]{:S(2)}, u32[]{:S(2)}) collective-permute-start(bf16[2048,2048]{1,0:T(8,128)(2,1)} %param.31), channel_id=1, source_target_pairs={{0,3},{1,0},{2,1},{3,2},{4,7},{5,4},{6,5},{7,6},{8,11},{9,8},{10,9... | collective-permute-start | bytes 25165832 | tf_op jit(solution)/shard_map/ppermute | solution.py:19
  417.8 512.9 %collective-permute-start.1 = (bf16[4096,2048]{1,0:T(8,128)(2,1)}, bf16[4096,2048]{1,0:T(8,128)(2,1)}, u32[]{:S(2)}, u32[]{:S(2)}) collective-permute-start(bf16[4096,2048]{1,0:T(8,128)(2,1)} %pad_maximum_fusion.1), channel_id=1, source_target_pairs={{0,2},{1,3},{2,0},{3,1},{4,6},{5,7},{6,4},{7,5},{8,10},{9,11},{10,... | collective-permute-start | bytes 50331656 | tf_op jit(solution)/shard_map/ppermute | solution.py:19
  419.3 1627.0 %reduce-scatter.10.cloned.1.call-start = ((), (), s32[]{:S(2)}) async-start(), calls=%async_computation.14 | async-start | bytes 9437184 | tf_op jit(solution)/shard_map/reduce_scatter | solution.py:319
  508.9 435.8 %copy-start.5 = (bf16[256,16,128]{0,2,1:T(8,128)(2,1)}, bf16[256,16,128]{0,2,1:T(8,128)(2,1)S(1)}, u32[]{:S(2)}) copy-start(bf16[256,16,128]{0,2,1:T(8,128)(2,1)S(1)} %maximum_convert_fusion) | copy-start | bytes 3145732
  1091.0 371.5 %copy-start.17 = (bf16[256,2048]{1,0:T(8,128)(2,1)}, bf16[256,2048]{1,0:T(8,128)(2,1)S(1)}, u32[]{:S(2)}) copy-start(bf16[256,2048]{1,0:T(8,128)(2,1)S(1)} %fusion.73) | copy-start | bytes 3145732
  1510.5 274.4 %copy-start.54 = (f32[256]{0:T(256)}, f32[256]{0:T(256)S(1)}, u32[]{:S(2)}) copy-start(f32[256]{0:T(256)S(1)} %multiply_multiply_fusion.8) | copy-start | bytes 3076
  1956.5 180.7 %reduce-scatter.12.cloned.1.call-start = ((), (), s32[]{:S(2)}) async-start(), calls=%async_computation.15 | async-start | bytes 9437184 | tf_op jit(solution)/shard_map/reduce_scatter | solution.py:322
  1957.3 469.9 %reduce-scatter.18.cloned.1.call-start = ((), (), s32[]{:S(2)}) async-start(), calls=%async_computation.18 | async-start | bytes 41943040
  1974.8 744.4 %reduce-scatter.14.cloned.1.call-start = ((), (), s32[]{:S(2)}) async-start(), calls=%async_computation.16 | async-start | bytes 41943040 | tf_op jit(solution)/shard_map/reduce_scatter | solution.py:345
  1977.9 69.8 %copy-start.33 = (f32[256,64]{0,1:T(8,128)S(1)}, f32[256,64]{0,1:T(8,128)}, u32[]{:S(2)}) copy-start(f32[256,64]{0,1:T(8,128)} %copy-done.32) | copy-start | bytes 196612
  2060.3 76.9 %copy-start.21 = (bf16[1,256,2048]{2,1,0:T(8,128)(2,1)S(1)}, bf16[1,256,2048]{2,1,0:T(8,128)(2,1)}, u32[]{:S(2)}) copy-start(bf16[1,256,2048]{2,1,0:T(8,128)(2,1)} %param.21) | copy-start | bytes 3145732
  2061.7 75.5 %copy-start.24 = (bf16[256,2048]{1,0:T(8,128)(2,1)S(1)}, bf16[256,2048]{1,0:T(8,128)(2,1)}, u32[]{:S(2)}) copy-start(bf16[256,2048]{1,0:T(8,128)(2,1)} %fusion.67) | copy-start | bytes 3145732
  2062.2 88.4 %copy-start.25 = (bf16[256,2048]{1,0:T(8,128)(2,1)}, bf16[256,2048]{1,0:T(8,128)(2,1)S(1)}, u32[]{:S(2)}) copy-start(bf16[256,2048]{1,0:T(8,128)(2,1)S(1)} %fusion.66) | copy-start | bytes 3145732
  2175.7 1104.7 %reduce-scatter.16.cloned.1.call-start = ((), (), s32[]{:S(2)}) async-start(), calls=%async_computation.17 | async-start | bytes 83886080
  2206.0 1728.9 %all-reduce.10.cloned.1.call-start = ((), (), s32[]{:S(2)}) async-start(), calls=%async_computation.19 | async-start | bytes 67108864 | tf_op jit(solution)/shard_map/psum | solution.py:355
  (66 other events, 574.2 us)
Sparse Core Ops, SparseCore 0:
  9.9 90.2 all-gather.14
  102.1 87.7 all-gather.18
  191.7 305.6 all-gather.22
  499.4 82.0 all-gather.16
  583.5 81.0 all-gather.20
  666.3 153.4 all-gather.24
  821.6 341.7 all-gather.26
  1165.2 297.2 all-gather.28
  1464.3 297.2 all-gather.30
  1956.7 89.5 reduce-scatter.9
  2049.2 87.9 reduce-scatter.11
  2140.1 286.9 reduce-scatter.17
  2430.5 288.5 reduce-scatter.13
  2722.0 558.2 reduce-scatter.15
  3283.1 651.7 all-reduce.9
